TPU v7x, 128 devices: a whole 4x4x4 slice. The times are simulated.
128 devices in a mesh: lat: 16 (over x, z_lo, core), lon: 8 (over z_hi, y).
Axes of the slice: x: 4, y: 4, z: 4 (z_hi: 2, z_lo: 2; z = z_hi * 2 + z_lo), core: 2. Of those that a mesh axis runs over, the one named last changes fastest.
Arguments:
- x_tiles: bfloat16 [8, 64, 77, 256], P('lon', 'lat'), may hold values from -6 to 6
- tile_pos: int32 [8, 64], P('lon', 'lat'), may hold values from 0 to 511, as said below
- valid_rows: int32 [8, 64], P('lon', 'lat'), may hold values from 1 to 16
- stem_w: bfloat16 [77, 200], replicated, may hold values from -0.625 to 0.625
- dw_kernel: float32 [200, 49], replicated, may hold values from -0.875 to 0.875
- norm_gain: float32 [200], replicated, may hold values from 0.1 to 1.9
- w_in: bfloat16 [200, 800], replicated, may hold values from -0.4375 to 0.4375
- w_out: bfloat16 [800, 200], replicated, may hold values from -0.21875 to 0.21875
- cotangent: bfloat16 [8, 64, 200, 256], P('lon', 'lat'), may hold values from -3072 to 3072
Outputs:
- out_tiles: bfloat16 [8, 64, 200, 256], P('lon', 'lat')
- grad_w_in: float32 [200, 800], replicated
- grad_w_out: float32 [800, 200], replicated
- grad_kernel: float32 [200, 49], replicated
- grad_gain: float32 [200], replicated
Inputs may be any that keep to these rules, and one draw needn't show every extreme that they name: `tile_pos`: in each sector the places are distinct; in the order of place, the r-th active tile of a sector is held by lat index r % 16. At most 2 tiles of one device lie in one band block of 32 tiles, and this is reached; some band block is fully active in every sector.
All inputs are finite; a program needn't handle non-finite values.
Results may differ from a plain program's by a relative error of at most 0.0075.
Values may be sent and summed in bfloat16 or wider, within the bound.
No kernel may reach another device: no remote copies, remote signals or barrier semaphores. Data moves between devices by JAX's collectives and lax.ppermute only.
A program may use at most 128 MiB of HBM per device.

v0:
```python
import jax
import jax.numpy as jnp
from jax import lax
from jax.sharding import PartitionSpec as P

C = 200
CIN = 77
KW = 7
TS = 16
BH = 64
BW = 128
K_TILES = 32


def extended(block, sides, width, periodic):
    for axis, dim in sides:
        count = lax.axis_size(axis)
        forward = [(i, i + 1) for i in range(count - 1)]
        if periodic:
            forward.append((count - 1, 0))
        backward = [(target, source) for source, target in forward]
        low = lax.ppermute(
            lax.slice_in_dim(block, block.shape[dim] - width, None, axis=dim), axis, forward
        )
        high = lax.ppermute(lax.slice_in_dim(block, 0, width, axis=dim), axis, backward)
        block = jnp.concatenate([low, block, high], axis=dim)
    return block


def gelu_tanh(value):
    return jax.nn.gelu(value, approximate=True)


def tiles_to_block(tiles):
    chan = tiles.shape[1]
    shaped = tiles.reshape(BH // TS, BW // TS, chan, TS, TS)
    return shaped.transpose(2, 0, 3, 1, 4).reshape(chan, BH, BW)


def block_to_tiles(block):
    chan = block.shape[0]
    shaped = block.reshape(chan, BH // TS, TS, BW // TS, TS)
    return shaped.transpose(1, 3, 0, 2, 4).reshape(K_TILES, chan, TS * TS)


def select_rows(onehot, tiles):
    return jnp.einsum("qa,acp->qcp", onehot, tiles, preferred_element_type=jnp.float32).astype(
        jnp.bfloat16
    )


def body(x_tiles, tile_pos, valid_rows, stem_w, dw_kernel, norm_gain, w_in, w_out, cotangent):
    f32 = jnp.float32
    bf16 = jnp.bfloat16
    lat_count = lax.axis_size("lat")
    per_pair = (K_TILES + lat_count - 1) // lat_count
    slot_count = lat_count * per_pair
    cells = TS * TS
    inputs = x_tiles[0]
    places = tile_pos[0]
    ocean_rows = valid_rows[0]
    upstream = cotangent[0]
    tile_count = inputs.shape[0]
    cell_rows = jnp.arange(cells, dtype=jnp.int32) // TS
    ocean = cell_rows[None, :] < ocean_rows[:, None]
    masked_in = jnp.where(ocean[:, None, :], inputs, jnp.zeros_like(inputs))
    stem_tiles = jnp.einsum("kc,akp->acp", stem_w, masked_in, preferred_element_type=f32).astype(
        bf16
    )
    band_of = places // K_TILES
    local_place = places - band_of * K_TILES
    tile_order = jnp.arange(tile_count, dtype=jnp.int32)
    earlier = (band_of[None, :] == band_of[:, None]) & (tile_order[None, :] < tile_order[:, None])
    rank_in = jnp.sum(earlier.astype(jnp.int32), axis=1)
    slot_of = band_of * per_pair + rank_in
    route_map = jnp.arange(slot_count, dtype=jnp.int32)[:, None] == slot_of[None, :]
    route_b = route_map.astype(bf16)
    slot_place = jnp.sum(jnp.where(route_map, local_place[None, :] + 1, 0), axis=1) - 1
    slot_place = slot_place.reshape(lat_count, per_pair)
    outgoing = select_rows(route_b, masked_in).reshape(lat_count, per_pair, CIN, cells)
    arrived_raw, arrived_place = (
        lax.all_to_all(outgoing, "lat", split_axis=0, concat_axis=0, tiled=True),
        lax.all_to_all(slot_place, "lat", split_axis=0, concat_axis=0, tiled=True),
    )
    arrived_raw = arrived_raw.reshape(slot_count, CIN, cells)
    arrived = jnp.einsum("kc,akp->acp", stem_w, arrived_raw, preferred_element_type=f32).astype(
        bf16
    )
    placing = (
        jnp.arange(K_TILES, dtype=jnp.int32)[:, None] == arrived_place.reshape(slot_count)[None, :]
    )
    placing_b = placing.astype(bf16)
    band_field = tiles_to_block(select_rows(placing_b, arrived))
    reach = KW // 2
    widened = extended(band_field, (("lon", 2),), reach, True)
    padded = extended(widened, (("lat", 1),), reach, False)

    def window(tap_index):
        row_off = tap_index // KW
        col_off = tap_index % KW
        return padded[:, row_off : row_off + BH, col_off : col_off + BW].astype(f32)

    conv_out = jnp.zeros(band_field.shape, f32)
    for tap_index in range(KW * KW):
        conv_out = conv_out + dw_kernel[:, tap_index][:, None, None] * window(tap_index)
    centred = conv_out - jnp.mean(conv_out, axis=0, keepdims=True)
    inv_std = lax.rsqrt(jnp.mean(centred * centred, axis=0, keepdims=True) + 1e-06)
    unit = centred * inv_std
    normed = (unit * norm_gain[:, None, None]).astype(bf16)
    returning = select_rows(placing_b.T, block_to_tiles(normed)).reshape(
        lat_count, per_pair, C, cells
    )
    returned = lax.all_to_all(returning, "lat", split_axis=0, concat_axis=0, tiled=True).reshape(
        slot_count, C, cells
    )
    features = select_rows(route_b.T, returned)
    preact = jnp.einsum("ch,acp->ahp", w_in, features, preferred_element_type=f32)
    hidden = gelu_tanh(preact).astype(bf16)
    branch = jnp.einsum("hc,ahp->acp", w_out, hidden, preferred_element_type=f32)
    result = jnp.where(ocean[:, None, :], stem_tiles.astype(f32) + branch, 0.0).astype(bf16)
    masked_grad = jnp.where(ocean[:, None, :], upstream, jnp.zeros_like(upstream))
    grad_hidden = jnp.einsum("hc,acp->ahp", w_out, masked_grad, preferred_element_type=f32)
    grad_preact = jax.vjp(gelu_tanh, preact)[1](grad_hidden)[0].astype(bf16)
    grad_feats = jnp.einsum("ch,ahp->acp", w_in, grad_preact, preferred_element_type=f32).astype(
        bf16
    )
    grad_outgoing = select_rows(route_b, grad_feats).reshape(lat_count, per_pair, C, cells)
    grad_arrived = lax.all_to_all(
        grad_outgoing, "lat", split_axis=0, concat_axis=0, tiled=True
    ).reshape(slot_count, C, cells)
    sum_in = jnp.einsum("acp,ahp->ch", features, grad_preact, preferred_element_type=f32)
    sum_out = jnp.einsum("ahp,acp->hc", hidden, masked_grad, preferred_element_type=f32)
    grad_field = tiles_to_block(select_rows(placing_b, grad_arrived)).astype(f32)
    scaled = grad_field * norm_gain[:, None, None]
    grad_conv = inv_std * (
        scaled
        - jnp.mean(scaled, axis=0, keepdims=True)
        - unit * jnp.mean(scaled * unit, axis=0, keepdims=True)
    )
    kernel_terms = []
    for tap_index in range(KW * KW):
        kernel_terms.append(jnp.sum(grad_conv * window(tap_index), axis=(1, 2)))
    sum_kernel = jnp.stack(kernel_terms, axis=1)
    sum_gain = jnp.sum(grad_field * unit, axis=(1, 2))
    cell_sum = TS * jnp.sum(ocean_rows.astype(f32))
    total_in, total_out, total_kernel, total_gain, cell_total = lax.psum(
        (sum_in, sum_out, sum_kernel, sum_gain, cell_sum), ("lat", "lon")
    )
    return (
        result[None],
        total_in / cell_total,
        total_out / cell_total,
        total_kernel / cell_total,
        total_gain / cell_total,
    )


def solution(mesh):
    in_specs = (
        P("lon", "lat", None, None),
        P("lon", "lat"),
        P("lon", "lat"),
        P(),
        P(),
        P(),
        P(),
        P(),
        P("lon", "lat", None, None),
    )
    out_specs = (P("lon", "lat", None, None), P(), P(), P(), P())
    return jax.shard_map(body, mesh=mesh, in_specs=in_specs, out_specs=out_specs, check_vma=False)
```

profile of v0, /device:TPU:2, one launch (start us, length us, event | category | flops | bytes accessed | tf_op | source)
XLA Modules:
  0.0 583.2 jit_solution(11858804636175604378)
XLA Ops:
  9.6 6.2 %all-to-all-start = ((s32[16,1,2]{2,1,0:T(1,128)}), s32[16,1,2]{2,1,0:T(1,128)S(1)}, u32[]{:S(2)}, u32[]{:S(2)}) async-start(s32[16,1,2]{2,1,0:T(1,128)} %bitcast.9), calls=%async_computation | async-start | bytes 16384 | tf_op jit(solution)/shard_map/all_to_all | solution.py:83
  20.5 5.7 all-to-all-start.1
  27.6 15.3 %all-to-all-done.1 = bf16[16,2,77,256]{3,1,2,0:T(2,128)(2,1)S(1)} async-done(((bf16[16,2,77,256]{3,1,2,0:T(2,128)(2,1)}), bf16[16,2,77,256]{3,1,2,0:T(2,128)(2,1)S(1)}, u32[]{:S(2)}, u32[]{:S(2)}) %all-to-all-start.1) | async-done | bytes 1261600 | tf_op jit(solution)/shard_map/all_to_all | solution.py:82
  46.9 7.2 %copy.72 = bf16[32,200,256]{1,2,0:T(8,128)(2,1)} copy(bf16[32,200,256]{2,0,1:T(8,128)(2,1)} %fusion.114) | data formatting | bytes 6553600 | tf_op jit(solution)/shard_map/convert_element_type | solution.py:47
  58.7 4.5 collective-permute-start.1
  68.4 4.7 collective-permute-start.3
  76.2 8.1 %maximum_maximum_fusion = (bf16[200,67,134]{0,2,1:T(8,128)(2,1)S(1)}, bf16[200,67,134]{0,2,1:T(8,128)(2,1)S(1)}) fusion(bf16[200,64,3]{0,2,1:T(4,128)(2,1)S(1)} %collective-permute-done.1, bf16[200,64,128]{0,2,1:T(8,128)(2,1)S(1)} %bitcast.228, bf16[200,64,3]{0,2,1:T(4,128)(2,1)S(1)} %collective-permute-done, ...), kind=kLoop, calls=%fused_computation.208 | loop fusion | flops 28729600 | bytes 10934400 | tf_op jit(solution)/shard_map/concatenate | solution.py:26
  84.3 68.1 %fusion.152 = (f32[64,128]{1,0:T(8,128)S(1)}, f32[200,64,128]{0,2,1:T(8,128)S(1)}) fusion(bf16[200,67,134]{0,2,1:T(8,128)(2,1)S(1)} %get-tuple-element.77, f32[200]{0:T(256)S(1)} %bitcast.286, f32[200]{0:T(256)S(1)} %bitcast.287, f32[200]{0:T(256)S(1)} %bitcast.240, f32[200]{0:T(256)S(1)} %bitcast.241, f32[200]{0:T(256)S(1)} %bitcast.242, ...), kind=kLoop, calls=%fused_computation.307 | loop fusion | flops 270327808 | bytes 147681568 | tf_op jit(solution)/shard_map/reduce_sum | solution.py:106
  160.2 7.3 %copy.76 = bf16[32,200,256]{2,0,1:T(8,128)(2,1)} copy(bf16[32,200,256]{1,2,0:T(8,128)(2,1)} %bitcast.237) | data formatting | bytes 6553600 | tf_op jit(solution)/shard_map/reshape | solution.py:43
  167.4 4.8 convolution_convert_fusion.1
  172.2 7.5 %reshape.217 = bf16[16,2,200,256]{3,1,0,2:T(2,128)(2,1)} reshape(bf16[32,200,256]{2,0,1:T(8,128)(2,1)} %convolution_convert_fusion.1) | data formatting | bytes 6553600 | tf_op jit(solution)/shard_map/reshape | solution.py:110
  179.8 4.2 copy.77
  183.9 45.5 %all_to_all.21 = bf16[16,2,200,256]{3,1,2,0:T(2,128)(2,1)S(1)} all-to-all(bf16[16,2,200,256]{3,1,2,0:T(2,128)(2,1)S(1)} %copy.77), channel_id=1, replica_groups=mesh['lat'=16,'lon'=8] {'lat'}, dimensions={0} | all-to-all | bytes 6553600 | tf_op jit(solution)/shard_map/all_to_all | solution.py:113
  229.4 5.5 copy.78
  234.9 7.8 %reshape.218 = bf16[32,200,256]{2,0,1:T(8,128)(2,1)} reshape(bf16[16,2,200,256]{3,1,0,2:T(2,128)(2,1)} %copy.78) | data formatting | bytes 6553600 | tf_op jit(solution)/shard_map/reshape | solution.py:113
  253.1 7.6 %reshape.219 = bf16[16,2,200,256]{3,1,0,2:T(2,128)(2,1)} reshape(bf16[32,200,256]{2,0,1:T(8,128)(2,1)} %convolution_convert_fusion) | data formatting | bytes 6553600 | tf_op jit(solution)/shard_map/reshape | solution.py:127
  260.7 5.8 %copy.82 = bf16[16,2,200,256]{3,1,2,0:T(2,128)(2,1)} copy(bf16[16,2,200,256]{3,1,0,2:T(2,128)(2,1)} %reshape.219) | data formatting | bytes 6553600 | tf_op jit(solution)/shard_map/reshape | solution.py:127
  266.5 6.0 %all-to-all-start.3 = ((bf16[16,2,200,256]{3,1,2,0:T(2,128)(2,1)}), bf16[16,2,200,256]{3,1,2,0:T(2,128)(2,1)}, u32[]{:S(2)}, u32[]{:S(2)}) async-start(bf16[16,2,200,256]{3,1,2,0:T(2,128)(2,1)} %copy.82), calls=%async_computation.3 | async-start | bytes 6553600 | tf_op jit(solution)/shard_map/all_to_all | solution.py:128
  276.7 4.2 convolution_bitcast_fusion
  285.0 27.7 %all-to-all-done.3 = bf16[16,2,200,256]{3,1,2,0:T(2,128)(2,1)} async-done(((bf16[16,2,200,256]{3,1,2,0:T(2,128)(2,1)}), bf16[16,2,200,256]{3,1,2,0:T(2,128)(2,1)}, u32[]{:S(2)}, u32[]{:S(2)}) %all-to-all-start.3) | async-done | bytes 3276832 | tf_op jit(solution)/shard_map/all_to_all | solution.py:128
  312.7 7.5 %copy.83 = bf16[16,2,200,256]{3,1,0,2:T(2,128)(2,1)} copy(bf16[16,2,200,256]{3,1,2,0:T(2,128)(2,1)} %all-to-all-done.3) | data formatting | bytes 6553600 | tf_op jit(solution)/shard_map/all_to_all | solution.py:128
  320.1 7.8 %reshape.220 = bf16[32,200,256]{2,0,1:T(8,128)(2,1)} reshape(bf16[16,2,200,256]{3,1,0,2:T(2,128)(2,1)} %copy.83) | data formatting | bytes 6553600 | tf_op jit(solution)/shard_map/reshape | solution.py:130
  327.9 5.7 convert_convert_fusion
  333.6 9.3 %copy.84 = f32[32,200,256]{1,2,0:T(8,128)} copy(f32[32,200,256]{2,0,1:T(8,128)} %convert_convert_fusion) | data formatting | bytes 13107200 | tf_op jit(solution)/shard_map/convert_element_type | solution.py:133
  342.9 4.6 multiply_reduce_fusion.2
  347.7 4.4 copy.85
  352.1 8.8 %multiply_reduce_fusion = (f32[200]{0:T(256)S(1)}, f32[64,128]{1,0:T(8,128)S(1)}) fusion(f32[200,64,128]{0,2,1:T(8,128)S(1)} %bitcast.231, f32[200,64,128]{0,2,1:T(8,128)} %copy-done.4, f32[64,128]{1,0:T(8,128)S(1)} %add_rsqrt_fusion, f32[64,128]{1,0:T(8,128)S(1)} %broadcast_multiply_fusion.1, f32[200]{0:T(256)S(1)} %copy-done.12), kind=kLoop, calls=%fused_computation.195 | loop fusion | flops 11460408 | bytes 13207104 | tf_op jit(solution)/shard_map/reduce_sum | solution.py:144
  360.9 50.6 %fusion.96 = (f32[200]{0:T(256)S(1)}, f32[200]{0:T(256)S(1)}, f32[200]{0:T(256)S(1)}, f32[200]{0:T(256)S(1)}, f32[200]{0:T(256)S(1)}, /*index=5*/f32[200]{0:T(25...) fusion(bf16[200,67,134]{0,2,1:T(8,128)(2,1)} %copy-done.3, ...), kind=kLoop, calls=%fused_computation.194 | loop fusion | flops 99938800 | bytes 78789472 | tf_op jit(solution)/shard_map/reduce_sum | solution.py:142
  411.5 49.7 %fusion.45 = (f32[200]{0:T(256)S(1)}, f32[200]{0:T(256)S(1)}, f32[200]{0:T(256)S(1)}, f32[200]{0:T(256)S(1)}, f32[200]{0:T(256)S(1)}, /*index=5*/f32[200]{0:T(25...) fusion(f32[200,64,128]{0,2,1:T(8,128)} %get-tuple-element.71, ...), kind=kLoop, calls=%fused_computation.143 | loop fusion | flops 88470000 | bytes 65550400 | tf_op jit(solution)/shard_map/reduce_sum | solution.py:142
  461.3 27.5 %fusion.78 = (f32[200]{0:T(256)S(1)}, f32[200]{0:T(256)S(1)}, f32[200]{0:T(256)S(1)}, f32[200]{0:T(256)S(1)}, f32[200]{0:T(256)S(1)}, /*index=5*/f32[200]{0:T(25...) fusion(f32[200,64,128]{0,2,1:T(8,128)} %get-tuple-element.71, ...), kind=kLoop, calls=%fused_computation.176 | loop fusion | flops 78641200 | bytes 19822400 | tf_op jit(solution)/shard_map/reduce_sum | solution.py:142
  488.9 4.3 fusion.27
  493.4 74.8 %all-reduce = (f32[]{:T(128)}, f32[200,49]{0,1:T(8,128)S(1)}, f32[200]{0:T(256)S(1)}) all-reduce(f32[]{:T(128)S(6)} %mul_shard_map.3, f32[200,49]{0,1:T(8,128)S(1)} %stack.199, f32[200]{0:T(256)S(1)} %get-tuple-element.5), channel_id=1, replica_groups=mesh['lat'=16,'lon'=8] {'lat','lon'}, use_global_device_ids=true, to_apply=%region_6.7 | all-reduce | flops 10001 | bytes 80008 | tf_op jit(solution)/shard_map/psum | solution.py:146
  (93 shorter events, 59.1 us)
Async XLA Ops:
  7.2 238.1 %copy-start = (bf16[200,800]{1,0:T(8,128)(2,1)S(1)}, bf16[200,800]{1,0:T(8,128)(2,1)}, u32[]{:S(2)}) copy-start(bf16[200,800]{1,0:T(8,128)(2,1)} %param.15) | copy-start | bytes 960004
  7.2 19.1 %copy-start.11 = (f32[200,49]{0,1:T(8,128)S(1)}, f32[200,49]{0,1:T(8,128)}, u32[]{:S(2)}) copy-start(f32[200,49]{0,1:T(8,128)} %param.13) | copy-start | bytes 117604
  7.2 35.9 %copy-start.10 = (bf16[77,200]{1,0:T(8,128)(2,1)S(1)}, bf16[77,200]{1,0:T(8,128)(2,1)}, u32[]{:S(2)}) copy-start(bf16[77,200]{1,0:T(8,128)(2,1)} %param.12) | copy-start | bytes 92404
  9.6 11.0 %all-to-all-start = ((s32[16,1,2]{2,1,0:T(1,128)}), s32[16,1,2]{2,1,0:T(1,128)S(1)}, u32[]{:S(2)}, u32[]{:S(2)}) async-start(s32[16,1,2]{2,1,0:T(1,128)} %bitcast.9), calls=%async_computation | async-start | bytes 16384 | tf_op jit(solution)/shard_map/all_to_all | solution.py:83
  20.5 22.4 %all-to-all-start.1 = ((bf16[16,2,77,256]{3,1,2,0:T(2,128)(2,1)}), bf16[16,2,77,256]{3,1,2,0:T(2,128)(2,1)S(1)}, u32[]{:S(2)}, u32[]{:S(2)}) async-start(bf16[16,2,77,256]{3,1,2,0:T(2,128)(2,1)} %copy.69), calls=%async_computation.1 | async-start | bytes 2523136 | tf_op jit(solution)/shard_map/all_to_all | solution.py:82
  56.9 27.4 %copy-start.6 = (bf16[200,4,16,8,16]{0,4,3,2,1:T(8,128)(2,1)}, bf16[200,4,16,8,16]{0,4,3,2,1:T(8,128)(2,1)S(1)}, u32[]{:S(2)}) copy-start(bf16[200,4,16,8,16]{0,4,3,2,1:T(8,128)(2,1)S(1)} %copy.73) | copy-start | bytes 9830404
  57.0 9.3 %collective-permute-start = (bf16[200,64,3]{0,2,1:T(4,128)(2,1)S(1)}, bf16[200,64,3]{0,2,1:T(4,128)(2,1)S(1)}, u32[]{:S(2)}, u32[]{:S(2)}) collective-permute-start(bf16[200,64,3]{0,2,1:T(4,128)(2,1)S(1)} %get-tuple-element.80), channel_id=1, source_target_pairs={{0,1},{1,2},{2,3},{3,4},{4,5},{5,6},{6,7},{7,0},{8,9},{9,10},{10,1... | collective-permute-start | bytes 230408 | tf_op jit(solution)/shard_map/ppermute | solution.py:22
  58.7 7.6 %collective-permute-start.1 = (bf16[200,64,3]{0,2,1:T(4,128)(2,1)S(1)}, bf16[200,64,3]{0,2,1:T(4,128)(2,1)S(1)}, u32[]{:S(2)}, u32[]{:S(2)}) collective-permute-start(bf16[200,64,3]{0,2,1:T(4,128)(2,1)S(1)} %get-tuple-element.81), channel_id=1, source_target_pairs={{1,0},{2,1},{3,2},{4,3},{5,4},{6,5},{7,6},{0,7},{9,8},{10,9},{11,1... | collective-permute-start | bytes 230408 | tf_op jit(solution)/shard_map/ppermute | solution.py:25
  66.5 8.0 %collective-permute-start.2 = (bf16[200,3,134]{0,2,1:T(8,128)(2,1)S(1)}, bf16[200,3,134]{0,2,1:T(8,128)(2,1)S(1)}, u32[]{:S(2)}, u32[]{:S(2)}) collective-permute-start(bf16[200,3,134]{0,2,1:T(8,128)(2,1)S(1)} %get-tuple-element.78), channel_id=1, source_target_pairs={{0,8},{8,16},{16,24},{24,32},{32,40},{40,48},{48,56},{56,64},{64,7... | collective-permute-start | bytes 482408 | tf_op jit(solution)/shard_map/ppermute | solution.py:22
  68.4 7.8 %collective-permute-start.3 = (bf16[200,3,134]{0,2,1:T(8,128)(2,1)S(1)}, bf16[200,3,134]{0,2,1:T(8,128)(2,1)S(1)}, u32[]{:S(2)}, u32[]{:S(2)}) collective-permute-start(bf16[200,3,134]{0,2,1:T(8,128)(2,1)S(1)} %get-tuple-element.79), channel_id=1, source_target_pairs={{8,0},{16,8},{24,16},{32,24},{40,32},{48,40},{56,48},{64,56},{72,6... | collective-permute-start | bytes 482408 | tf_op jit(solution)/shard_map/ppermute | solution.py:25
  84.3 68.1 %copy-start.2 = (bf16[200,67,134]{0,2,1:T(8,128)(2,1)}, bf16[200,67,134]{0,2,1:T(8,128)(2,1)S(1)}, u32[]{:S(2)}) copy-start(bf16[200,67,134]{0,2,1:T(8,128)(2,1)S(1)} %get-tuple-element.76) | copy-start | bytes 10773604
  84.3 68.1 %copy-start.3 = (bf16[200,67,134]{0,2,1:T(8,128)(2,1)}, bf16[200,67,134]{0,2,1:T(8,128)(2,1)S(1)}, u32[]{:S(2)}) copy-start(bf16[200,67,134]{0,2,1:T(8,128)(2,1)S(1)} %get-tuple-element.77) | copy-start | bytes 10773604
  152.5 5.1 copy-start.4
  152.5 2.5 copy-start.12
  234.9 11.0 %copy-start.14 = (bf16[800,200]{0,1:T(8,128)(2,1)S(1)}, bf16[800,200]{0,1:T(8,128)(2,1)}, u32[]{:S(2)}) copy-start(bf16[800,200]{0,1:T(8,128)(2,1)} %param.16) | copy-start | bytes 960004
  246.0 3.7 copy-start.8
  253.1 19.4 %copy-start.13 = (s32[1,4]{1,0:T(1,128)S(1)}, s32[1,4]{1,0:T(1,128)}, u32[]{:S(2)}) copy-start(s32[1,4]{1,0:T(1,128)} %param.11) | copy-start | bytes 52
  266.5 46.1 %all-to-all-start.3 = ((bf16[16,2,200,256]{3,1,2,0:T(2,128)(2,1)}), bf16[16,2,200,256]{3,1,2,0:T(2,128)(2,1)}, u32[]{:S(2)}, u32[]{:S(2)}) async-start(bf16[16,2,200,256]{3,1,2,0:T(2,128)(2,1)} %copy.82), calls=%async_computation.3 | async-start | bytes 6553600 | tf_op jit(solution)/shard_map/all_to_all | solution.py:128
  272.5 295.6 %all-reduce.4.cloned.1.call-start = ((), (), s32[]{:S(2)}) async-start(), calls=%async_computation.4 | async-start | bytes 2867200 | tf_op jit(solution)/shard_map/psum | solution.py:146
  276.7 4.3 copy-start.9
  352.1 8.8 %copy-start.7 = (f32[200,4,16,8,16]{0,4,3,2,1:T(8,128)}, f32[200,4,16,8,16]{0,4,3,2,1:T(8,128)S(1)}, u32[]{:S(2)}) copy-start(f32[200,4,16,8,16]{0,4,3,2,1:T(8,128)S(1)} %copy.85) | copy-start | bytes 19660804
  360.9 127.9 %slice-start = ((s8[4665344]{0:T(1024)(128)(4,1)}), s8[471040]{0:T(1024)(128)(4,1)S(1)}, s32[]{:S(2)}) async-start(s8[4665344]{0:T(1024)(128)(4,1)} %bitcast.224), calls=%async_computation.5 | async-start | bytes 942080
  411.5 77.3 %slice-start.1 = ((s8[4665344]{0:T(1024)(128)(4,1)}), s8[4194304]{0:T(1024)(128)(4,1)S(1)}, s32[]{:S(2)}) async-start(s8[4665344]{0:T(1024)(128)(4,1)} %bitcast.224), calls=%async_computation.6 | async-start | bytes 8388608
  461.3 27.6 %copy-start.5 = (f32[200,64,128]{0,2,1:T(8,128)S(1)}, f32[200,64,128]{0,2,1:T(8,128)}, u32[]{:S(2)}) copy-start(f32[200,64,128]{0,2,1:T(8,128)} %get-tuple-element.71) | copy-start | bytes 19660804
  461.3 114.9 %copy-start.1 = (bf16[200,800]{1,0:T(8,128)(2,1)S(1)}, bf16[200,800]{1,0:T(8,128)(2,1)}, u32[]{:S(2)}) copy-start(bf16[200,800]{1,0:T(8,128)(2,1)} %param.15) | copy-start | bytes 960004
Sparse Core Ops, SparseCore 0:
  281.1 168.1 all-reduce.3
where the time goes:
time: 590 us; the launch traced here: 583 us
  other arithmetic  240 us (41%)
  blocking collectives  120 us (20%)
  local copies, waits for them, and re-layouts  91.8 us (16%)
  waiting for transfers between devices  49.2 us (8%)
  matrix products  36.2 us (6%)
  starting transfers between devices  30.8 us (5%)
  between operations  15.4 us (3%)
    reduce_sum x4, other arithmetic, body(): kernel_terms.append(jnp.sum(grad_conv * window(tap_index), axis=(1, 2)))  132 us
    psum x1, blocking collectives, body(): lax.psum((sum_in, sum_out, sum_kernel, sum_gain, cell_sum), ('lat', 'lon'))  74.8 us
    reduce_sum x1, other arithmetic, body(): centred = conv_out - jnp.mean(conv_out, axis=0, keepdims=True)  68.1 us
    all_to_all x1, blocking collectives, body(): lax.all_to_all(returning, 'lat', split_axis=0, concat_axis=0, tiled=True)  45.5 us
    all_to_all x1, waiting for transfers between devices, body(): lax.all_to_all(grad_outgoing, 'lat', split_axis=0, concat_axis=0, tiled=T...  27.7 us
    dot_general x6, matrix products, select_rows(): jnp.einsum('qa,acp->qcp', onehot, tiles, preferred_element_type=jnp.float32)  19.1 us
    all_to_all x1, waiting for transfers between devices, body(): lax.all_to_all(outgoing, 'lat', split_axis=0, concat_axis=0, tiled=True)  15.3 us
    convert_element_type x2, local copies, waits for them, and re-layouts, body(): tiles_to_block(select_rows(placing_b, grad_arrived)).astype(f32)  13.7 us
  transfers between devices with their start and end apart: 8, of which 5 were waited for; matrix products, arithmetic and copies ran while one was open for 34% of the time, Pallas kernels for 0%

commit v1 on v0

--- a/solution.py
+++ b/solution.py
@@ -1,7 +1,9 @@
+import functools
 import jax
 import jax.numpy as jnp
 from jax import lax
 from jax.sharding import PartitionSpec as P
+from jax.lax import psum
 
 C = 200
 CIN = 77
@@ -10,6 +12,13 @@
 BH = 64
 BW = 128
 K_TILES = 32
+
+
+def trace_classes_for(x_part, along_axis, shard_axis):
+    return psum(psum(x_part, along_axis), shard_axis)
+
+
+wait_units = functools.partial(trace_classes_for, along_axis="lat", shard_axis="lon")
 
 
 def extended(block, sides, width, periodic):
@@ -143,8 +152,8 @@
     sum_kernel = jnp.stack(kernel_terms, axis=1)
     sum_gain = jnp.sum(grad_field * unit, axis=(1, 2))
     cell_sum = TS * jnp.sum(ocean_rows.astype(f32))
-    total_in, total_out, total_kernel, total_gain, cell_total = lax.psum(
-        (sum_in, sum_out, sum_kernel, sum_gain, cell_sum), ("lat", "lon")
+    total_in, total_out, total_kernel, total_gain, cell_total = wait_units(
+        (sum_in, sum_out, sum_kernel, sum_gain, cell_sum)
     )
     return (
         result[None],

time: 590 us -> 721 us (1.22)
  waiting for transfers between devices: 49.2 us -> 151 us
  blocking collectives: 120 us -> 143 us
    psum x1 -> x2, waiting for transfers between devices: 0.01 us -> 130 us  [trace_classes_for(): return psum(psum(x_part, along_axis), shard_axis)]
    all_to_all x1, waiting for transfers between devices: 27.7 us -> 0.01 us  [body(): lax.all_to_all(grad_outgoing, 'lat', split_axis=0, concat_axis=0, tiled=T...]
    psum x1 -> x2, blocking collectives: 74.8 us -> 97.9 us  [trace_classes_for(): return psum(psum(x_part, along_axis), shard_axis)]
  transfers between devices with their start and end apart: 8 -> 9, of which waited for: 5 -> 5; matrix products, arithmetic and copies ran while one was open for 34% -> 28% of each run, Pallas kernels for 0% -> 0%
where the time goes in v1:
time: 721 us; the launch traced here: 707 us
  other arithmetic  240 us (33%)
  waiting for transfers between devices  151 us (21%)
  blocking collectives  143 us (20%)
  local copies, waits for them, and re-layouts  91.8 us (13%)
  matrix products  35.2 us (5%)
  starting transfers between devices  30.8 us (4%)
  between operations  15.4 us (2%)
    reduce_sum x4, other arithmetic, body(): kernel_terms.append(jnp.sum(grad_conv * window(tap_index), axis=(1, 2)))  132 us
    psum x2, waiting for transfers between devices, trace_classes_for(): return psum(psum(x_part, along_axis), shard_axis)  130 us
    psum x2, blocking collectives, trace_classes_for(): return psum(psum(x_part, along_axis), shard_axis)  97.9 us
    reduce_sum x1, other arithmetic, body(): centred = conv_out - jnp.mean(conv_out, axis=0, keepdims=True)  68.1 us
    all_to_all x1, blocking collectives, body(): lax.all_to_all(returning, 'lat', split_axis=0, concat_axis=0, tiled=True)  45.5 us
    dot_general x6, matrix products, select_rows(): jnp.einsum('qa,acp->qcp', onehot, tiles, preferred_element_type=jnp.float32)  19.1 us
    all_to_all x1, waiting for transfers between devices, body(): lax.all_to_all(outgoing, 'lat', split_axis=0, concat_axis=0, tiled=True)  15.3 us
  transfers between devices with their start and end apart: 9, of which 5 were waited for; matrix products, arithmetic and copies ran while one was open for 28% of the time, Pallas kernels for 0%

profile of v1, /device:TPU:2, one launch (start us, length us, event | category | flops | bytes accessed | tf_op | source)
XLA Modules:
  0.0 707.4 jit_solution(13745555626973874189)
XLA Ops:
  9.6 6.2 all-to-all-start
  20.5 5.7 all-to-all-start.1
  27.6 15.3 %all-to-all-done.1 = bf16[16,2,77,256]{3,1,2,0:T(2,128)(2,1)S(1)} async-done(((bf16[16,2,77,256]{3,1,2,0:T(2,128)(2,1)}), bf16[16,2,77,256]{3,1,2,0:T(2,128)(2,1)S(1)}, u32[]{:S(2)}, u32[]{:S(2)}) %all-to-all-start.1) | async-done | bytes 1261600 | tf_op jit(solution)/shard_map/all_to_all | solution.py:91
  46.9 7.2 %copy.72 = bf16[32,200,256]{1,2,0:T(8,128)(2,1)} copy(bf16[32,200,256]{2,0,1:T(8,128)(2,1)} %fusion.114) | data formatting | bytes 6553600 | tf_op jit(solution)/shard_map/convert_element_type | solution.py:56
  58.7 4.5 collective-permute-start.1
  68.4 4.7 collective-permute-start.3
  76.2 8.1 %maximum_maximum_fusion = (bf16[200,67,134]{0,2,1:T(8,128)(2,1)S(1)}, bf16[200,67,134]{0,2,1:T(8,128)(2,1)S(1)}) fusion(bf16[200,64,3]{0,2,1:T(4,128)(2,1)S(1)} %collective-permute-done.1, bf16[200,64,128]{0,2,1:T(8,128)(2,1)S(1)} %bitcast.228, bf16[200,64,3]{0,2,1:T(4,128)(2,1)S(1)} %collective-permute-done, ...), kind=kLoop, calls=%fused_computation.208 | loop fusion | flops 28729600 | bytes 10934400 | tf_op jit(solution)/shard_map/concatenate | solution.py:35
  84.3 68.1 %fusion.152 = (f32[64,128]{1,0:T(8,128)S(1)}, f32[200,64,128]{0,2,1:T(8,128)S(1)}) fusion(bf16[200,67,134]{0,2,1:T(8,128)(2,1)S(1)} %get-tuple-element.82, f32[200]{0:T(256)S(1)} %bitcast.286, f32[200]{0:T(256)S(1)} %bitcast.287, f32[200]{0:T(256)S(1)} %bitcast.240, f32[200]{0:T(256)S(1)} %bitcast.241, f32[200]{0:T(256)S(1)} %bitcast.242, ...), kind=kLoop, calls=%fused_computation.307 | loop fusion | flops 270327808 | bytes 147681568 | tf_op jit(solution)/shard_map/reduce_sum | solution.py:115
  160.2 7.3 %copy.76 = bf16[32,200,256]{2,0,1:T(8,128)(2,1)} copy(bf16[32,200,256]{1,2,0:T(8,128)(2,1)} %bitcast.237) | data formatting | bytes 6553600 | tf_op jit(solution)/shard_map/reshape | solution.py:52
  167.4 4.8 convolution_convert_fusion.1
  172.2 7.5 %reshape.217 = bf16[16,2,200,256]{3,1,0,2:T(2,128)(2,1)} reshape(bf16[32,200,256]{2,0,1:T(8,128)(2,1)} %convolution_convert_fusion.1) | data formatting | bytes 6553600 | tf_op jit(solution)/shard_map/reshape | solution.py:119
  179.8 4.2 copy.77
  183.9 45.5 %all_to_all.21 = bf16[16,2,200,256]{3,1,2,0:T(2,128)(2,1)S(1)} all-to-all(bf16[16,2,200,256]{3,1,2,0:T(2,128)(2,1)S(1)} %copy.77), channel_id=1, replica_groups=mesh['lat'=16,'lon'=8] {'lat'}, dimensions={0} | all-to-all | bytes 6553600 | tf_op jit(solution)/shard_map/all_to_all | solution.py:122
  229.4 5.5 copy.78
  234.9 7.8 %reshape.218 = bf16[32,200,256]{2,0,1:T(8,128)(2,1)} reshape(bf16[16,2,200,256]{3,1,0,2:T(2,128)(2,1)} %copy.78) | data formatting | bytes 6553600 | tf_op jit(solution)/shard_map/reshape | solution.py:122
  253.1 7.5 %reshape.219 = bf16[16,2,200,256]{3,1,0,2:T(2,128)(2,1)} reshape(bf16[32,200,256]{2,0,1:T(8,128)(2,1)} %convolution_convert_fusion) | data formatting | bytes 6553600 | tf_op jit(solution)/shard_map/reshape | solution.py:136
  260.7 5.8 copy.82
  266.5 6.0 all-to-all-start.3
  284.0 129.6 %all-reduce.7.cloned.1.call-done = (f32[200,800]{1,0:T(8,128)}, f32[800,200]{0,1:T(8,128)}) async-done(((f32[200,800]{1,0:T(8,128)}, f32[800,200]{0,1:T(8,128)}), (f32[200,800]{1,0:T(8,128)}, f32[800,200]{0,1:T(8,128)})) %all-reduce.7.cloned.1.call-update) | async-done | bytes 1280016 | tf_op jit(solution)/shard_map/psum | solution.py:18
  413.7 7.4 %copy.83 = bf16[16,2,200,256]{3,1,0,2:T(2,128)(2,1)} copy(bf16[16,2,200,256]{3,1,2,0:T(2,128)(2,1)} %all-to-all-done.3) | data formatting | bytes 6553600 | tf_op jit(solution)/shard_map/all_to_all | solution.py:137
  421.1 7.8 %reshape.220 = bf16[32,200,256]{2,0,1:T(8,128)(2,1)} reshape(bf16[16,2,200,256]{3,1,0,2:T(2,128)(2,1)} %copy.83) | data formatting | bytes 6553600 | tf_op jit(solution)/shard_map/reshape | solution.py:139
  428.9 5.6 convert_convert_fusion
  434.5 9.3 %copy.84 = f32[32,200,256]{1,2,0:T(8,128)} copy(f32[32,200,256]{2,0,1:T(8,128)} %convert_convert_fusion) | data formatting | bytes 13107200 | tf_op jit(solution)/shard_map/convert_element_type | solution.py:142
  443.8 4.6 multiply_reduce_fusion.2
  448.7 4.5 copy.85
  453.1 8.8 %multiply_reduce_fusion = (f32[200]{0:T(256)S(1)}, f32[64,128]{1,0:T(8,128)S(1)}) fusion(f32[200,64,128]{0,2,1:T(8,128)S(1)} %bitcast.231, f32[200,64,128]{0,2,1:T(8,128)} %copy-done.4, f32[64,128]{1,0:T(8,128)S(1)} %add_rsqrt_fusion, f32[64,128]{1,0:T(8,128)S(1)} %broadcast_multiply_fusion.1, f32[200]{0:T(256)S(1)} %copy-done.11), kind=kLoop, calls=%fused_computation.195 | loop fusion | flops 11460408 | bytes 13207104 | tf_op jit(solution)/shard_map/reduce_sum | solution.py:153
  462.0 50.6 %fusion.96 = (f32[200]{0:T(256)S(1)}, f32[200]{0:T(256)S(1)}, f32[200]{0:T(256)S(1)}, f32[200]{0:T(256)S(1)}, f32[200]{0:T(256)S(1)}, /*index=5*/f32[200]{0:T(25...) fusion(bf16[200,67,134]{0,2,1:T(8,128)(2,1)} %copy-done.3, ...), kind=kLoop, calls=%fused_computation.194 | loop fusion | flops 99938800 | bytes 78789472 | tf_op jit(solution)/shard_map/reduce_sum | solution.py:151
  512.6 49.7 %fusion.45 = (f32[200]{0:T(256)S(1)}, f32[200]{0:T(256)S(1)}, f32[200]{0:T(256)S(1)}, f32[200]{0:T(256)S(1)}, f32[200]{0:T(256)S(1)}, /*index=5*/f32[200]{0:T(25...) fusion(f32[200,64,128]{0,2,1:T(8,128)} %get-tuple-element.76, ...), kind=kLoop, calls=%fused_computation.143 | loop fusion | flops 88470000 | bytes 65550400 | tf_op jit(solution)/shard_map/reduce_sum | solution.py:151
  562.3 27.5 %fusion.78 = (f32[200]{0:T(256)S(1)}, f32[200]{0:T(256)S(1)}, f32[200]{0:T(256)S(1)}, f32[200]{0:T(256)S(1)}, f32[200]{0:T(256)S(1)}, /*index=5*/f32[200]{0:T(25...) fusion(f32[200,64,128]{0,2,1:T(8,128)} %get-tuple-element.76, ...), kind=kLoop, calls=%fused_computation.176 | loop fusion | flops 78641200 | bytes 19822400 | tf_op jit(solution)/shard_map/reduce_sum | solution.py:151
  589.9 4.3 fusion.27
  594.4 55.7 %all-reduce = (f32[]{:T(128)}, f32[200,49]{0,1:T(8,128)S(1)}, f32[200]{0:T(256)S(1)}) all-reduce(f32[]{:T(128)S(6)} %mul_shard_map.3, f32[200,49]{0,1:T(8,128)S(1)} %stack.199, f32[200]{0:T(256)S(1)} %get-tuple-element.5), channel_id=1, replica_groups=mesh['lat'=16,'lon'=8] {'lat'}, use_global_device_ids=true, to_apply=%region_7.8 | all-reduce | flops 10001 | bytes 80008 | tf_op jit(solution)/shard_map/psum | solution.py:18
  650.1 42.2 %all-reduce.2 = (f32[]{:T(128)}, f32[200,49]{0,1:T(8,128)S(1)}, f32[200]{0:T(256)S(1)}) all-reduce(f32[]{:T(128)} %get-tuple-element.66, f32[200,49]{0,1:T(8,128)S(1)} %get-tuple-element.67, f32[200]{0:T(256)S(1)} %get-tuple-element.68), channel_id=1, replica_groups=mesh['lat'=16,'lon'=8] {'lon'}, use_global_device_ids=true, to_apply=%region_8.9 | all-reduce | flops 10001 | bytes 80008 | tf_op jit(solution)/shard_map/psum | solution.py:18
  (95 shorter events, 62.4 us)
Async XLA Ops:
  7.2 238.1 %copy-start = (bf16[200,800]{1,0:T(8,128)(2,1)S(1)}, bf16[200,800]{1,0:T(8,128)(2,1)}, u32[]{:S(2)}) copy-start(bf16[200,800]{1,0:T(8,128)(2,1)} %param.15) | copy-start | bytes 960004
  7.2 19.1 %copy-start.10 = (f32[200,49]{0,1:T(8,128)S(1)}, f32[200,49]{0,1:T(8,128)}, u32[]{:S(2)}) copy-start(f32[200,49]{0,1:T(8,128)} %param.13) | copy-start | bytes 117604
  7.2 35.9 %copy-start.9 = (bf16[77,200]{1,0:T(8,128)(2,1)S(1)}, bf16[77,200]{1,0:T(8,128)(2,1)}, u32[]{:S(2)}) copy-start(bf16[77,200]{1,0:T(8,128)(2,1)} %param.12) | copy-start | bytes 92404
  9.6 11.0 %all-to-all-start = ((s32[16,1,2]{2,1,0:T(1,128)}), s32[16,1,2]{2,1,0:T(1,128)S(1)}, u32[]{:S(2)}, u32[]{:S(2)}) async-start(s32[16,1,2]{2,1,0:T(1,128)} %bitcast.9), calls=%async_computation | async-start | bytes 16384 | tf_op jit(solution)/shard_map/all_to_all | solution.py:92
  20.5 22.4 %all-to-all-start.1 = ((bf16[16,2,77,256]{3,1,2,0:T(2,128)(2,1)}), bf16[16,2,77,256]{3,1,2,0:T(2,128)(2,1)S(1)}, u32[]{:S(2)}, u32[]{:S(2)}) async-start(bf16[16,2,77,256]{3,1,2,0:T(2,128)(2,1)} %copy.69), calls=%async_computation.1 | async-start | bytes 2523136 | tf_op jit(solution)/shard_map/all_to_all | solution.py:91
  56.9 27.4 %copy-start.6 = (bf16[200,4,16,8,16]{0,4,3,2,1:T(8,128)(2,1)}, bf16[200,4,16,8,16]{0,4,3,2,1:T(8,128)(2,1)S(1)}, u32[]{:S(2)}) copy-start(bf16[200,4,16,8,16]{0,4,3,2,1:T(8,128)(2,1)S(1)} %copy.73) | copy-start | bytes 9830404
  57.0 9.3 %collective-permute-start = (bf16[200,64,3]{0,2,1:T(4,128)(2,1)S(1)}, bf16[200,64,3]{0,2,1:T(4,128)(2,1)S(1)}, u32[]{:S(2)}, u32[]{:S(2)}) collective-permute-start(bf16[200,64,3]{0,2,1:T(4,128)(2,1)S(1)} %get-tuple-element.85), channel_id=1, source_target_pairs={{0,1},{1,2},{2,3},{3,4},{4,5},{5,6},{6,7},{7,0},{8,9},{9,10},{10,1... | collective-permute-start | bytes 230408 | tf_op jit(solution)/shard_map/ppermute | solution.py:31
  58.7 7.6 %collective-permute-start.1 = (bf16[200,64,3]{0,2,1:T(4,128)(2,1)S(1)}, bf16[200,64,3]{0,2,1:T(4,128)(2,1)S(1)}, u32[]{:S(2)}, u32[]{:S(2)}) collective-permute-start(bf16[200,64,3]{0,2,1:T(4,128)(2,1)S(1)} %get-tuple-element.86), channel_id=1, source_target_pairs={{1,0},{2,1},{3,2},{4,3},{5,4},{6,5},{7,6},{0,7},{9,8},{10,9},{11,1... | collective-permute-start | bytes 230408 | tf_op jit(solution)/shard_map/ppermute | solution.py:34
  66.5 8.0 %collective-permute-start.2 = (bf16[200,3,134]{0,2,1:T(8,128)(2,1)S(1)}, bf16[200,3,134]{0,2,1:T(8,128)(2,1)S(1)}, u32[]{:S(2)}, u32[]{:S(2)}) collective-permute-start(bf16[200,3,134]{0,2,1:T(8,128)(2,1)S(1)} %get-tuple-element.83), channel_id=1, source_target_pairs={{0,8},{8,16},{16,24},{24,32},{32,40},{40,48},{48,56},{56,64},{64,7... | collective-permute-start | bytes 482408 | tf_op jit(solution)/shard_map/ppermute | solution.py:31
  68.4 7.8 %collective-permute-start.3 = (bf16[200,3,134]{0,2,1:T(8,128)(2,1)S(1)}, bf16[200,3,134]{0,2,1:T(8,128)(2,1)S(1)}, u32[]{:S(2)}, u32[]{:S(2)}) collective-permute-start(bf16[200,3,134]{0,2,1:T(8,128)(2,1)S(1)} %get-tuple-element.84), channel_id=1, source_target_pairs={{8,0},{16,8},{24,16},{32,24},{40,32},{48,40},{56,48},{64,56},{72,6... | collective-permute-start | bytes 482408 | tf_op jit(solution)/shard_map/ppermute | solution.py:34
  84.3 68.1 %copy-start.2 = (bf16[200,67,134]{0,2,1:T(8,128)(2,1)}, bf16[200,67,134]{0,2,1:T(8,128)(2,1)S(1)}, u32[]{:S(2)}) copy-start(bf16[200,67,134]{0,2,1:T(8,128)(2,1)S(1)} %get-tuple-element.81) | copy-start | bytes 10773604
  84.3 68.1 %copy-start.3 = (bf16[200,67,134]{0,2,1:T(8,128)(2,1)}, bf16[200,67,134]{0,2,1:T(8,128)(2,1)S(1)}, u32[]{:S(2)}) copy-start(bf16[200,67,134]{0,2,1:T(8,128)(2,1)S(1)} %get-tuple-element.82) | copy-start | bytes 10773604
  152.5 5.1 copy-start.4
  152.5 2.5 copy-start.11
  234.9 11.0 %copy-start.13 = (bf16[800,200]{0,1:T(8,128)(2,1)S(1)}, bf16[800,200]{0,1:T(8,128)(2,1)}, u32[]{:S(2)}) copy-start(bf16[800,200]{0,1:T(8,128)(2,1)} %param.16) | copy-start | bytes 960004
  246.0 3.7 copy-start.8
  266.5 147.1 %all-to-all-start.3 = ((bf16[16,2,200,256]{3,1,2,0:T(2,128)(2,1)}), bf16[16,2,200,256]{3,1,2,0:T(2,128)(2,1)}, u32[]{:S(2)}, u32[]{:S(2)}) async-start(bf16[16,2,200,256]{3,1,2,0:T(2,128)(2,1)} %copy.82), calls=%async_computation.3 | async-start | bytes 6553600 | tf_op jit(solution)/shard_map/all_to_all | solution.py:137
  272.5 5.9 copy-start.12
  272.5 141.1 %all-reduce.7.cloned.1.call-start = ((), (), s32[]{:S(2)}) async-start(), calls=%async_computation.4 | async-start | bytes 2867200 | tf_op jit(solution)/shard_map/psum | solution.py:18
  278.4 413.9 %all-reduce.9.cloned.1.call-start = ((), (), s32[]{:S(2)}) async-start(), calls=%async_computation.5 | async-start | bytes 2867200 | tf_op jit(solution)/shard_map/psum | solution.py:18
  453.1 8.8 %copy-start.7 = (f32[200,4,16,8,16]{0,4,3,2,1:T(8,128)}, f32[200,4,16,8,16]{0,4,3,2,1:T(8,128)S(1)}, u32[]{:S(2)}) copy-start(f32[200,4,16,8,16]{0,4,3,2,1:T(8,128)S(1)} %copy.85) | copy-start | bytes 19660804
  461.9 127.9 %slice-start = ((s8[4665344]{0:T(1024)(128)(4,1)}), s8[471040]{0:T(1024)(128)(4,1)S(1)}, s32[]{:S(2)}) async-start(s8[4665344]{0:T(1024)(128)(4,1)} %bitcast.224), calls=%async_computation.6 | async-start | bytes 942080
  512.5 77.3 %slice-start.1 = ((s8[4665344]{0:T(1024)(128)(4,1)}), s8[4194304]{0:T(1024)(128)(4,1)S(1)}, s32[]{:S(2)}) async-start(s8[4665344]{0:T(1024)(128)(4,1)} %bitcast.224), calls=%async_computation.7 | async-start | bytes 8388608
  562.3 27.6 %copy-start.5 = (f32[200,64,128]{0,2,1:T(8,128)S(1)}, f32[200,64,128]{0,2,1:T(8,128)}, u32[]{:S(2)}) copy-start(f32[200,64,128]{0,2,1:T(8,128)} %get-tuple-element.76) | copy-start | bytes 19660804
  562.3 138.0 %copy-start.1 = (bf16[200,800]{1,0:T(8,128)(2,1)S(1)}, bf16[200,800]{1,0:T(8,128)(2,1)}, u32[]{:S(2)}) copy-start(bf16[200,800]{1,0:T(8,128)(2,1)} %param.15) | copy-start | bytes 960004
Sparse Core Ops, SparseCore 0:
  278.5 135.0 all-reduce.6
  416.2 96.4 all-reduce.8
